TPU v7x, 256 devices: a whole 4x4x8 slice. The times are simulated.
256 devices in a mesh: replica: 16 (over z, core), tile: 16 (over x, y).
Axes of the slice: x: 4, y: 4, z: 8, core: 2. Of those that a mesh axis runs over, the one named last changes fastest.
Arguments:
- public_tokens: bfloat16 [4096, 5120], P('replica', 'tile'), may hold values from -6 to 6
- public_targets: bfloat16 [4096, 4096], P(('replica', 'tile')), may hold values from -6 to 6
- private_tokens: bfloat16 [6144, 5120], P('replica', 'tile'), may hold values from -6 to 6
- private_targets: bfloat16 [6144, 4096], P(('replica', 'tile')), may hold values from -6 to 6
- token_counts: int32 [16, 3], P('replica'), may hold values from 1 to 128, 320 in all within a row
- weight: float32 [5120, 4096], P('tile', 'replica'), may hold values from -0.078125 to 0.078125
- public_moment: float32 [5120, 4096], P('tile', 'replica'), may hold values from 1 to 10
- adam_first: float32 [5120, 4096], P('tile', 'replica'), may hold values from -3 to 3
- adam_second: float32 [5120, 4096], P('tile', 'replica'), may hold values from 0.1 to 1
- noise_draw: float32 [5120, 4096], P('tile', 'replica'), may hold values from -6 to 6
Outputs:
- new_weight: float32 [5120, 4096], P('tile', 'replica')
- new_first: float32 [5120, 4096], P('tile', 'replica')
- new_second: float32 [5120, 4096], P('tile', 'replica')
- new_public: float32 [5120, 4096], P('tile', 'replica')
Inputs may be any that keep to these rules, and one draw needn't show every extreme that they name: `token_counts`: each row holds the live token counts of one replica's 3 private examples; every row sums to 320 and its largest entry is 128.
All inputs are finite; a program needn't handle non-finite values.
Results may differ from a plain program's by a relative error of at most 0.0031.
Values may be sent and summed in bfloat16 or wider, within the bound.
No kernel may reach another device: no remote copies, remote signals or barrier semaphores. Data moves between devices by JAX's collectives and lax.ppermute only.
A program may use at most 64 MiB of HBM per device.

v0:
```python
import math
import jax
import jax.numpy as jnp
from jax import lax
from jax.sharding import PartitionSpec as P

D = 5120
L = 128
Q = 4096
beta_first = 0.9
beta_second = 0.99
beta_public = 0.9
public_epsilon = 0.001
adam_epsilon = 1e-08
clip_factor = 0.6
noise_level = 4.0
learn_rate = 0.01
contract_rows = (((0,), (0,)), ((), ()))


def slot_owner(first_row, span, seq_len):
    rows_at = first_row + jnp.arange(span, dtype=jnp.int32)
    return (rows_at, rows_at // seq_len)


def per_slot(owners, values):
    picks = jnp.arange(values.shape[0], dtype=jnp.int32)
    return jnp.sum(jnp.where(owners[:, None] == picks[None, :], values[None, :], 0), axis=1)


def live_slots(first_row, span, counts_row, seq_len):
    rows_at, owners = slot_owner(first_row, span, seq_len)
    return rows_at % seq_len < per_slot(owners, counts_row)


def on_device(
    public_tokens,
    public_targets,
    private_tokens,
    private_targets,
    token_counts,
    weight,
    public_moment,
    adam_first,
    adam_second,
    noise_draw,
):
    replicas = lax.axis_size("replica")
    tile_pos = lax.axis_index("tile")
    seq_len = L
    w_half = lax.all_gather(weight.astype(jnp.bfloat16), "replica", axis=1, tiled=True)
    public_total = public_tokens.shape[0] * replicas
    block_x = public_tokens
    public_out = lax.psum_scatter(
        jnp.dot(block_x, w_half, preferred_element_type=jnp.float32),
        "tile",
        scatter_dimension=0,
        tiled=True,
    )
    public_delta = (public_out - public_targets.astype(jnp.float32)).astype(jnp.bfloat16)
    block_x = public_tokens
    public_grad = lax.dot_general(
        block_x,
        lax.all_gather(public_delta, "tile", axis=0, tiled=True),
        contract_rows,
        preferred_element_type=jnp.float32,
    )
    grad_owned = lax.psum_scatter(
        public_grad, "replica", scatter_dimension=1, tiled=True
    ) / math.sqrt(public_total)
    new_public = beta_public * public_moment + (1.0 - beta_public) * grad_owned * grad_owned
    precond_owned = 1.0 / (jnp.sqrt(new_public) + public_epsilon)
    precond = lax.all_gather(precond_owned, "replica", axis=1, tiled=True)
    counts_row = token_counts[0]
    slots_all = private_tokens.shape[0]
    slot_rows = private_targets.shape[0]
    block_x = private_tokens
    private_out = lax.psum_scatter(
        jnp.dot(block_x, w_half, preferred_element_type=jnp.float32),
        "tile",
        scatter_dimension=0,
        tiled=True,
    )
    local_live = live_slots(tile_pos * slot_rows, slot_rows, counts_row, seq_len)
    local_delta = jnp.where(
        local_live[:, None], private_out - private_targets.astype(jnp.float32), 0.0
    ).astype(jnp.bfloat16)
    private_delta = lax.all_gather(local_delta, "tile", axis=0, tiled=True)

    def example_norm(example):
        first_row = example * seq_len
        block_x = lax.dynamic_slice_in_dim(private_tokens, first_row, seq_len, 0)
        block_d = lax.dynamic_slice_in_dim(private_delta, first_row, seq_len, 0)
        grads = lax.dot_general(block_x, block_d, contract_rows, preferred_element_type=jnp.float32)
        scaled = grads * precond
        return jnp.sum(scaled * scaled)

    examples_here = token_counts.shape[1]
    partial_norms = lax.map(example_norm, jnp.arange(examples_here, dtype=jnp.int32))
    squares = lax.psum(partial_norms, "tile")
    clip_norm = clip_factor * math.sqrt(L * D * Q)
    factors = clip_norm / jnp.maximum(jnp.sqrt(squares), clip_norm)
    rows_at, owners = slot_owner(0, slots_all, seq_len)
    slot_factor = per_slot(owners, factors)
    weighted = (slot_factor[:, None] * private_delta.astype(jnp.float32)).astype(jnp.bfloat16)
    summed = precond * lax.dot_general(
        private_tokens, weighted, contract_rows, preferred_element_type=jnp.float32
    )
    summed_owned = lax.psum_scatter(summed, "replica", scatter_dimension=1, tiled=True)
    examples_total = examples_here * replicas
    noise_scale = noise_level * clip_factor * math.sqrt(L)
    gradient = (summed_owned + noise_scale * noise_draw) / examples_total
    new_first = beta_first * adam_first + (1.0 - beta_first) * gradient
    new_second = beta_second * adam_second + (1.0 - beta_second) * gradient * gradient
    first_hat = new_first / (1.0 - beta_first**2)
    second_hat = new_second / (1.0 - beta_second**2)
    new_weight = weight - learn_rate * first_hat / (jnp.sqrt(second_hat) + adam_epsilon)
    return (new_weight, new_first, new_second, new_public)


def solution(mesh):
    placed = (
        P("replica", "tile"),
        P(("replica", "tile"), None),
        P("replica", "tile"),
        P(("replica", "tile"), None),
        P("replica", None),
        P("tile", "replica"),
        P("tile", "replica"),
        P("tile", "replica"),
        P("tile", "replica"),
        P("tile", "replica"),
    )
    return jax.shard_map(
        on_device,
        mesh=mesh,
        in_specs=placed,
        out_specs=(
            P("tile", "replica"),
            P("tile", "replica"),
            P("tile", "replica"),
            P("tile", "replica"),
        ),
        check_vma=False,
    )
```

profile of v0, /device:TPU:2, one launch (start us, length us, event | category | flops | bytes accessed | tf_op | source)
XLA Modules:
  0.0 588.4 jit_solution(9840578557947384932)
XLA Ops:
  7.2 1.7 convert_element_type.23
  9.0 46.8 %all-gather.5.cloned.1.call-done = bf16[320,4096]{1,0:T(8,128)(2,1)} async-done(((bf16[320,256]{1,0:T(8,128)(2,1)}), bf16[320,4096]{1,0:T(8,128)(2,1)}) %all-gather.5.cloned.1.call-update) | async-done | bytes 2621456 | tf_op jit(solution)/shard_map/all_gather | solution.py:51
  55.8 5.2 fusion.11
  61.1 82.5 %reduce-scatter.7.cloned.1.call-done = f32[16,4096]{1,0:T(8,128)} async-done(((f32[256,4096]{1,0:T(8,128)}), f32[16,4096]{1,0:T(8,128)}) %reduce-scatter.7.cloned.1.call-update) | async-done | bytes 262160 | tf_op jit(solution)/shard_map/reduce_scatter | solution.py:54
  143.6 1.6 subtract_convert_fusion
  145.3 4.5 fusion.12
  149.9 45.9 %all-gather.7.cloned.1.call-done = bf16[256,4096]{1,0:T(8,128)(2,1)} async-done(((bf16[16,4096]{1,0:T(8,128)(2,1)}), bf16[256,4096]{1,0:T(8,128)(2,1)}) %all-gather.7.cloned.1.call-update) | async-done | bytes 2097168 | tf_op jit(solution)/shard_map/all_gather | solution.py:64
  195.8 4.8 convolution_bitcast_fusion.1
  201.4 84.1 %reduce-scatter.13.cloned.1.call-done = f32[24,4096]{1,0:T(8,128)} async-done(((f32[384,4096]{1,0:T(8,128)}), f32[24,4096]{1,0:T(8,128)}) %reduce-scatter.13.cloned.1.call-update) | async-done | bytes 393232
  285.5 1.8 select_convert_fusion
  287.3 65.5 %reduce-scatter.9.cloned.1.call-done = f32[320,256]{1,0:T(8,128)} async-done(((f32[320,4096]{1,0:T(8,128)}), f32[320,256]{1,0:T(8,128)}) %reduce-scatter.9.cloned.1.call-update) | async-done | bytes 327696 | tf_op jit(solution)/shard_map/reduce_scatter | solution.py:68
  352.8 1.9 add_divide_fusion
  354.8 51.4 %all-gather.11.cloned.1.call-done = bf16[384,4096]{1,0:T(8,128)(2,1)} async-done(((bf16[24,4096]{1,0:T(8,128)(2,1)}), bf16[384,4096]{1,0:T(8,128)(2,1)}) %all-gather.11.cloned.1.call-update) | async-done | bytes 3145744 | tf_op jit(solution)/shard_map/all_gather | solution.py:88
  406.3 45.5 %all-gather.9.cloned.1.call-done = f32[320,4096]{1,0:T(8,128)} async-done(((f32[320,256]{1,0:T(8,128)}), f32[320,4096]{1,0:T(8,128)}) %all-gather.9.cloned.1.call-update) | async-done | bytes 5242896 | tf_op jit(solution)/shard_map/all_gather | solution.py:73
  451.7 20.8 %while.10 = (s32[]{:T(128)}, f32[3]{0:T(128)S(1)}, s32[3]{0:T(128)S(1)}, bf16[384,320]{0,1:T(8,128)(2,1)S(1)}, bf16[384,4096]{1,0:T(8,128)(2,1)}, /*index=5*/f32...) while((s32[]{:T(128)}, f32[3]{0:T(128)S(1)}, s32[3]{0:T(128)S(1)}, ...), condition=%wide.region_6.7_spmd, body=%wide.region_4.6_spmd.sunk | while | flops 339476480 | bytes 6374575 | solution.py:99
  453.0 4.9 fusion.25
  457.9 0.8 dynamic_update_slice.5
  459.9 5.0 fusion.25
  464.9 0.8 dynamic_update_slice.5
  466.9 5.0 fusion.25
  472.6 34.3 %psum.7 = f32[3]{0:T(128)S(1)} all-reduce(f32[3]{0:T(128)S(1)} %get-tuple-element.36), channel_id=1, replica_groups=mesh['replica'=16,'tile'=16] {'tile'}, use_global_device_ids=true, to_apply=%region_7.8 | all-reduce | flops 3 | bytes 24 | tf_op jit(solution)/shard_map/psum | solution.py:100
  506.9 7.4 %fusion.5 = f32[320,4096]{1,0:T(8,128)} fusion(f32[320,4096]{1,0:T(8,128)} %get-tuple-element.130, bf16[384,320]{0,1:T(8,128)(2,1)S(1)} %get-tuple-element.142, bf16[384,4096]{1,0:T(8,128)(2,1)} %get-tuple-element.138, f32[384]{0:T(512)S(1)} %select_reduce_fusion), kind=kOutput, calls=%fused_computation.9 | convolution fusion | flops 1012662272 | bytes 13878784 | tf_op jit(solution)/shard_map/dot_general | solution.py:106
  514.4 65.1 %reduce-scatter.11.cloned.1.call-done = f32[320,256]{1,0:T(8,128)} async-done(((f32[320,4096]{1,0:T(8,128)}), f32[320,256]{1,0:T(8,128)}) %reduce-scatter.11.cloned.1.call-update) | async-done | bytes 327696 | tf_op jit(solution)/shard_map/reduce_scatter | solution.py:109
  579.5 2.1 divide_subtract_fusion
  (50 shorter events, 3.8 us)
Async XLA Ops:
  7.2 48.6 %copy-start = (bf16[256,320]{0,1:T(8,128)(2,1)S(1)}, bf16[256,320]{0,1:T(8,128)(2,1)}, u32[]{:S(2)}) copy-start(bf16[256,320]{0,1:T(8,128)(2,1)} %param.12) | copy-start | bytes 491524
  7.2 48.6 %all-gather.5.cloned.1.call-start = ((), (), s32[]{:S(2)}) async-start(), calls=%async_computation.4 | async-start | bytes 2785280 | tf_op jit(solution)/shard_map/all_gather | solution.py:51
  8.9 134.6 %copy-start.9 = (bf16[16,4096]{1,0:T(8,128)(2,1)S(1)}, bf16[16,4096]{1,0:T(8,128)(2,1)}, u32[]{:S(2)}) copy-start(bf16[16,4096]{1,0:T(8,128)(2,1)} %param.13) | copy-start | bytes 393220
  9.0 136.3 %copy-start.2 = (bf16[384,320]{0,1:T(8,128)(2,1)S(1)}, bf16[384,320]{0,1:T(8,128)(2,1)}, u32[]{:S(2)}) copy-start(bf16[384,320]{0,1:T(8,128)(2,1)} %param.14) | copy-start | bytes 737284
  9.0 134.6 %reduce-scatter.7.cloned.1.call-start = ((), (), s32[]{:S(2)}) async-start(), calls=%async_computation.5 | async-start | bytes 4456448 | tf_op jit(solution)/shard_map/reduce_scatter | solution.py:54
  55.8 89.5 %copy-start.1 = (bf16[320,4096]{1,0:T(8,128)(2,1)S(1)}, bf16[320,4096]{1,0:T(8,128)(2,1)}, u32[]{:S(2)}) copy-start(bf16[320,4096]{1,0:T(8,128)(2,1)} %all-gather.5.cloned.1.call-done) | copy-start | bytes 7864324
  61.1 134.8 %all-gather.7.cloned.1.call-start = ((), (), s32[]{:S(2)}) async-start(), calls=%async_computation.6 | async-start | bytes 2228224 | tf_op jit(solution)/shard_map/all_gather | solution.py:64
  145.2 140.3 %reduce-scatter.13.cloned.1.call-start = ((), (), s32[]{:S(2)}) async-start(), calls=%async_computation.11 | async-start | bytes 6684672
  149.9 202.9 %reduce-scatter.9.cloned.1.call-start = ((), (), s32[]{:S(2)}) async-start(), calls=%async_computation.7 | async-start | bytes 5570560 | tf_op jit(solution)/shard_map/reduce_scatter | solution.py:68
  200.6 0.7 copy-start.10
  200.6 84.9 %copy-start.8 = (bf16[24,4096]{1,0:T(8,128)(2,1)S(1)}, bf16[24,4096]{1,0:T(8,128)(2,1)}, u32[]{:S(2)}) copy-start(bf16[24,4096]{1,0:T(8,128)(2,1)} %param.15) | copy-start | bytes 589828
  200.6 152.2 %copy-start.4 = (f32[320,256]{1,0:T(8,128)S(1)}, f32[320,256]{1,0:T(8,128)}, u32[]{:S(2)}) copy-start(f32[320,256]{1,0:T(8,128)} %param.18) | copy-start | bytes 983044
  200.6 205.6 %all-gather.11.cloned.1.call-start = ((), (), s32[]{:S(2)}) async-start(), calls=%async_computation.9 | async-start | bytes 3342336 | tf_op jit(solution)/shard_map/all_gather | solution.py:88
  287.3 164.4 %all-gather.9.cloned.1.call-start = ((), (), s32[]{:S(2)}) async-start(), calls=%async_computation.8 | async-start | bytes 5570560 | tf_op jit(solution)/shard_map/all_gather | solution.py:73
  354.8 224.7 %reduce-scatter.11.cloned.1.call-start = ((), (), s32[]{:S(2)}) async-start(), calls=%async_computation.10 | async-start | bytes 5570560 | tf_op jit(solution)/shard_map/reduce_scatter | solution.py:109
  514.3 65.2 %copy-start.3 = (f32[320,256]{1,0:T(8,128)S(1)}, f32[320,256]{1,0:T(8,128)}, u32[]{:S(2)}) copy-start(f32[320,256]{1,0:T(8,128)} %param.17) | copy-start | bytes 983044
  514.3 65.2 %copy-start.5 = (f32[320,256]{1,0:T(8,128)S(1)}, f32[320,256]{1,0:T(8,128)}, u32[]{:S(2)}) copy-start(f32[320,256]{1,0:T(8,128)} %param.21) | copy-start | bytes 983044
  514.3 65.2 %copy-start.6 = (f32[320,256]{1,0:T(8,128)S(1)}, f32[320,256]{1,0:T(8,128)}, u32[]{:S(2)}) copy-start(f32[320,256]{1,0:T(8,128)} %param.19) | copy-start | bytes 983044
  514.3 65.2 %copy-start.7 = (f32[320,256]{1,0:T(8,128)S(1)}, f32[320,256]{1,0:T(8,128)}, u32[]{:S(2)}) copy-start(f32[320,256]{1,0:T(8,128)} %param.20) | copy-start | bytes 983044
Sparse Core Ops, SparseCore 0:
  10.3 45.4 all-gather.4
  61.2 82.3 reduce-scatter.6
  146.6 49.2 all-gather.6
  199.4 86.0 reduce-scatter.12
  287.9 64.8 reduce-scatter.8
  355.7 50.5 all-gather.10
  408.7 42.9 all-gather.8
  514.5 64.9 reduce-scatter.10
where the time goes:
time: 589 us; the launch traced here: 588 us
  waiting for transfers between devices  487 us (83%)
  matrix products  36.8 us (6%)
  blocking collectives  34.3 us (6%)
  between operations  14.2 us (2%)
  other arithmetic  9.32 us (2%)
    unnamed x9, waiting for transfers between devices  84.3 us
    reduce_scatter x1, waiting for transfers between devices, on_device(): lax.psum_scatter(jnp.dot(block_x, w_half, preferred_element_type=jnp.floa...  82.5 us
    reduce_scatter x1, waiting for transfers between devices, on_device(): lax.psum_scatter(public_grad, 'replica', scatter_dimension=1, tiled=True)  65.5 us
    reduce_scatter x1, waiting for transfers between devices, on_device(): lax.psum_scatter(summed, 'replica', scatter_dimension=1, tiled=True)  65.1 us
    all_gather x1, waiting for transfers between devices, on_device(): private_delta = lax.all_gather(local_delta, 'tile', axis=0, tiled=True)  51.4 us
    all_gather x1, waiting for transfers between devices, on_device(): lax.all_gather(weight.astype(jnp.bfloat16), 'replica', axis=1, tiled=True)  46.8 us
    all_gather x1, waiting for transfers between devices, on_device(): lax.all_gather(public_delta, 'tile', axis=0, tiled=True)  45.9 us
    all_gather x1, waiting for transfers between devices, on_device(): precond = lax.all_gather(precond_owned, 'replica', axis=1, tiled=True)  45.5 us
  transfers between devices with their start and end apart: 8, of which 8 were waited for; matrix products, arithmetic and copies ran while one was open for 2% of the time, Pallas kernels for 0%

commit v1 on v0

--- a/solution.py
+++ b/solution.py
@@ -70,7 +70,10 @@
     ) / math.sqrt(public_total)
     new_public = beta_public * public_moment + (1.0 - beta_public) * grad_owned * grad_owned
     precond_owned = 1.0 / (jnp.sqrt(new_public) + public_epsilon)
-    precond = lax.all_gather(precond_owned, "replica", axis=1, tiled=True)
+    size = lax.axis_size("replica")
+    parts = jnp.stack([precond_owned for _ in range(size)])
+    parts = lax.all_to_all(parts, "replica", split_axis=0, concat_axis=0)
+    precond = jnp.concatenate(parts, axis=1)
     counts_row = token_counts[0]
     slots_all = private_tokens.shape[0]
     slot_rows = private_targets.shape[0]

time: 589 us -> 548 us (0.930)
  waiting for transfers between devices: 487 us -> 432 us
  local copies, waits for them, and re-layouts: 4.62 us -> 14.3 us
    all_gather x1 -> x0, waiting for transfers between devices: 45.5 us -> none  [on_device(): precond = lax.all_gather(precond_owned, 'replica', axis=1, tiled=True)]
    all_gather x1, waiting for transfers between devices: 51.4 us -> 11.3 us  [on_device(): private_delta = lax.all_gather(local_delta, 'tile', axis=0, tiled=True)]
    all_to_all x0 -> x1, waiting for transfers between devices: none -> 35.4 us  [on_device(): parts = lax.all_to_all(parts, 'replica', split_axis=0, concat_axis=0)]
    reduce_scatter x1, waiting for transfers between devices: 65.5 us -> 58.8 us  [on_device(): lax.psum_scatter(public_grad, 'replica', scatter_dimension=1, tiled=True)]
    unnamed x9 -> x8, waiting for transfers between devices: 84.3 us -> 79.4 us
  transfers between devices with their start and end apart: 8 -> 8, of which waited for: 8 -> 8; matrix products, arithmetic and copies ran while one was open for 2% -> 3% of each run, Pallas kernels for 0% -> 0%
where the time goes in v1:
time: 548 us; the launch traced here: 547 us
  waiting for transfers between devices  432 us (79%)
  matrix products  36.6 us (7%)
  blocking collectives  33.3 us (6%)
  local copies, waits for them, and re-layouts  14.3 us (3%)
  between operations  14.2 us (3%)
  other arithmetic  9.21 us (2%)
    reduce_scatter x1, waiting for transfers between devices, on_device(): lax.psum_scatter(jnp.dot(block_x, w_half, preferred_element_type=jnp.floa...  82.5 us
    unnamed x8, waiting for transfers between devices  79.4 us
    reduce_scatter x1, waiting for transfers between devices, on_device(): lax.psum_scatter(summed, 'replica', scatter_dimension=1, tiled=True)  67.7 us
    reduce_scatter x1, waiting for transfers between devices, on_device(): lax.psum_scatter(public_grad, 'replica', scatter_dimension=1, tiled=True)  58.8 us
    all_gather x1, waiting for transfers between devices, on_device(): lax.all_gather(public_delta, 'tile', axis=0, tiled=True)  50.6 us
    all_gather x1, waiting for transfers between devices, on_device(): lax.all_gather(weight.astype(jnp.bfloat16), 'replica', axis=1, tiled=True)  46.8 us
    all_to_all x1, waiting for transfers between devices, on_device(): parts = lax.all_to_all(parts, 'replica', split_axis=0, concat_axis=0)  35.4 us
    psum x1, blocking collectives, on_device(): squares = lax.psum(partial_norms, 'tile')  33.3 us
  transfers between devices with their start and end apart: 8, of which 8 were waited for; matrix products, arithmetic and copies ran while one was open for 3% of the time, Pallas kernels for 0%

profile of v1, /device:TPU:2, one launch (start us, length us, event | category | flops | bytes accessed | tf_op | source)
XLA Modules:
  0.0 547.0 jit_solution(4225169907690063380)
XLA Ops:
  7.2 1.7 convert_element_type.23
  9.0 46.8 %all-gather.4.cloned.1.call-done = bf16[320,4096]{1,0:T(8,128)(2,1)} async-done(((bf16[320,256]{1,0:T(8,128)(2,1)}), bf16[320,4096]{1,0:T(8,128)(2,1)}) %all-gather.4.cloned.1.call-update) | async-done | bytes 2621456 | tf_op jit(solution)/shard_map/all_gather | solution.py:51
  55.8 5.1 fusion.11
  60.9 82.5 %reduce-scatter.7.cloned.1.call-done = f32[16,4096]{1,0:T(8,128)} async-done(((f32[256,4096]{1,0:T(8,128)}), f32[16,4096]{1,0:T(8,128)}) %reduce-scatter.7.cloned.1.call-update) | async-done | bytes 262160 | tf_op jit(solution)/shard_map/reduce_scatter | solution.py:54
  145.1 50.6 %all-gather.6.cloned.1.call-done = bf16[256,4096]{1,0:T(8,128)(2,1)} async-done(((bf16[16,4096]{1,0:T(8,128)(2,1)}), bf16[256,4096]{1,0:T(8,128)(2,1)}) %all-gather.6.cloned.1.call-update) | async-done | bytes 2097168 | tf_op jit(solution)/shard_map/all_gather | solution.py:64
  195.7 4.8 convolution_bitcast_fusion.1
  202.2 4.5 fusion.12
  206.7 58.8 %reduce-scatter.9.cloned.1.call-done = f32[320,256]{1,0:T(8,128)} async-done(((f32[320,4096]{1,0:T(8,128)}), f32[320,256]{1,0:T(8,128)}) %reduce-scatter.9.cloned.1.call-update) | async-done | bytes 327696 | tf_op jit(solution)/shard_map/reduce_scatter | solution.py:68
  265.5 1.8 add_divide_fusion
  267.4 2.8 stack.2
  270.1 4.7 all-to-all-start
  275.1 79.3 %reduce-scatter.13.cloned.1.call-done = f32[24,4096]{1,0:T(8,128)} async-done(((f32[384,4096]{1,0:T(8,128)}), f32[24,4096]{1,0:T(8,128)}) %reduce-scatter.13.cloned.1.call-update) | async-done | bytes 393232
  354.4 1.8 select_convert_fusion
  356.2 35.4 %all-to-all-done = f32[16,320,256]{2,1,0:T(8,128)} async-done(((f32[16,320,256]{2,1,0:T(8,128)}), f32[16,320,256]{2,1,0:T(8,128)}, u32[]{:S(2)}, u32[]{:S(2)}) %all-to-all-start) | async-done | bytes 5242912 | tf_op jit(solution)/shard_map/all_to_all | solution.py:75
  391.6 5.8 %copy.16 = f32[16,40,8,256]{3,2,0,1:T(8,128)} copy(f32[16,40,8,256]{3,2,1,0:T(8,128)} %bitcast.7) | data formatting | bytes 10485760 | tf_op jit(solution)/shard_map/reshape | solution.py:76
  397.4 11.3 %all-gather.8.cloned.1.call-done = bf16[384,4096]{1,0:T(8,128)(2,1)} async-done(((bf16[24,4096]{1,0:T(8,128)(2,1)}), bf16[384,4096]{1,0:T(8,128)(2,1)}) %all-gather.8.cloned.1.call-update) | async-done | bytes 3145744 | tf_op jit(solution)/shard_map/all_gather | solution.py:91
  408.7 20.8 %while.10 = (s32[]{:T(128)}, f32[3]{0:T(128)S(1)}, s32[3]{0:T(128)S(1)}, bf16[384,320]{0,1:T(8,128)(2,1)S(1)}, bf16[384,4096]{1,0:T(8,128)(2,1)}, /*index=5*/f32...) while((s32[]{:T(128)}, f32[3]{0:T(128)S(1)}, s32[3]{0:T(128)S(1)}, ...), condition=%wide.region_6.7_spmd, body=%wide.region_4.6_spmd.sunk | while | flops 339476480 | bytes 6374575 | solution.py:102
  410.0 4.9 fusion.25
  416.9 5.0 fusion.25
  423.9 5.0 fusion.25
  429.6 33.3 %psum.7 = f32[3]{0:T(128)S(1)} all-reduce(f32[3]{0:T(128)S(1)} %get-tuple-element.36), channel_id=1, replica_groups=mesh['replica'=16,'tile'=16] {'tile'}, use_global_device_ids=true, to_apply=%region_7.8 | all-reduce | flops 3 | bytes 24 | tf_op jit(solution)/shard_map/psum | solution.py:103
  462.9 7.4 %fusion.5 = f32[320,4096]{1,0:T(8,128)} fusion(f32[320,4096]{1,0:T(8,128)} %get-tuple-element.128, bf16[384,320]{0,1:T(8,128)(2,1)S(1)} %get-tuple-element.142, bf16[384,4096]{1,0:T(8,128)(2,1)} %get-tuple-element.136, f32[384]{0:T(512)S(1)} %select_reduce_fusion), kind=kOutput, calls=%fused_computation.9 | convolution fusion | flops 1012662272 | bytes 13878784 | tf_op jit(solution)/shard_map/dot_general | solution.py:109
  470.4 67.7 %reduce-scatter.11.cloned.1.call-done = f32[320,256]{1,0:T(8,128)} async-done(((f32[320,4096]{1,0:T(8,128)}), f32[320,256]{1,0:T(8,128)}) %reduce-scatter.11.cloned.1.call-update) | async-done | bytes 327696 | tf_op jit(solution)/shard_map/reduce_scatter | solution.py:112
  538.1 2.1 divide_subtract_fusion
  (51 shorter events, 8.0 us)
Async XLA Ops:
  7.2 48.6 %copy-start = (bf16[256,320]{0,1:T(8,128)(2,1)S(1)}, bf16[256,320]{0,1:T(8,128)(2,1)}, u32[]{:S(2)}) copy-start(bf16[256,320]{0,1:T(8,128)(2,1)} %param.12) | copy-start | bytes 491524
  7.2 48.6 %all-gather.4.cloned.1.call-start = ((), (), s32[]{:S(2)}) async-start(), calls=%async_computation.5 | async-start | bytes 2785280 | tf_op jit(solution)/shard_map/all_gather | solution.py:51
  8.9 134.5 %copy-start.9 = (bf16[16,4096]{1,0:T(8,128)(2,1)S(1)}, bf16[16,4096]{1,0:T(8,128)(2,1)}, u32[]{:S(2)}) copy-start(bf16[16,4096]{1,0:T(8,128)(2,1)} %param.13) | copy-start | bytes 393220
  9.0 134.5 %reduce-scatter.7.cloned.1.call-start = ((), (), s32[]{:S(2)}) async-start(), calls=%async_computation.6 | async-start | bytes 4456448 | tf_op jit(solution)/shard_map/reduce_scatter | solution.py:54
  60.9 134.8 %all-gather.6.cloned.1.call-start = ((), (), s32[]{:S(2)}) async-start(), calls=%async_computation.7 | async-start | bytes 2228224 | tf_op jit(solution)/shard_map/all_gather | solution.py:64
  145.1 120.4 %reduce-scatter.9.cloned.1.call-start = ((), (), s32[]{:S(2)}) async-start(), calls=%async_computation.8 | async-start | bytes 5570560 | tf_op jit(solution)/shard_map/reduce_scatter | solution.py:68
  200.5 1.7 copy-start.1
  200.5 1.7 copy-start.2
  200.5 153.8 %reduce-scatter.13.cloned.1.call-start = ((), (), s32[]{:S(2)}) async-start(), calls=%async_computation.11 | async-start | bytes 6684672
  206.7 58.8 %copy-start.4 = (f32[320,256]{1,0:T(8,128)S(1)}, f32[320,256]{1,0:T(8,128)}, u32[]{:S(2)}) copy-start(f32[320,256]{1,0:T(8,128)} %param.18) | copy-start | bytes 983044
  270.1 4.8 copy-start.10
  270.1 84.2 %copy-start.8 = (bf16[24,4096]{1,0:T(8,128)(2,1)S(1)}, bf16[24,4096]{1,0:T(8,128)(2,1)}, u32[]{:S(2)}) copy-start(bf16[24,4096]{1,0:T(8,128)(2,1)} %param.15) | copy-start | bytes 589828
  270.1 121.5 %all-to-all-start = ((f32[16,320,256]{2,1,0:T(8,128)}), f32[16,320,256]{2,1,0:T(8,128)}, u32[]{:S(2)}, u32[]{:S(2)}) async-start(f32[16,320,256]{2,1,0:T(8,128)} %stack.2), calls=%async_computation.2 | async-start | bytes 10485760 | tf_op jit(solution)/shard_map/all_to_all | solution.py:75
  274.9 133.9 %all-gather.8.cloned.1.call-start = ((), (), s32[]{:S(2)}) async-start(), calls=%async_computation.9 | async-start | bytes 3342336 | tf_op jit(solution)/shard_map/all_gather | solution.py:91
  356.1 181.9 %reduce-scatter.11.cloned.1.call-start = ((), (), s32[]{:S(2)}) async-start(), calls=%async_computation.10 | async-start | bytes 5570560 | tf_op jit(solution)/shard_map/reduce_scatter | solution.py:112
  470.3 67.7 %copy-start.3 = (f32[320,256]{1,0:T(8,128)S(1)}, f32[320,256]{1,0:T(8,128)}, u32[]{:S(2)}) copy-start(f32[320,256]{1,0:T(8,128)} %param.17) | copy-start | bytes 983044
  470.4 67.7 %copy-start.5 = (f32[320,256]{1,0:T(8,128)S(1)}, f32[320,256]{1,0:T(8,128)}, u32[]{:S(2)}) copy-start(f32[320,256]{1,0:T(8,128)} %param.21) | copy-start | bytes 983044
  470.4 67.7 %copy-start.6 = (f32[320,256]{1,0:T(8,128)S(1)}, f32[320,256]{1,0:T(8,128)}, u32[]{:S(2)}) copy-start(f32[320,256]{1,0:T(8,128)} %param.19) | copy-start | bytes 983044
  470.4 67.7 %copy-start.7 = (f32[320,256]{1,0:T(8,128)S(1)}, f32[320,256]{1,0:T(8,128)}, u32[]{:S(2)}) copy-start(f32[320,256]{1,0:T(8,128)} %param.20) | copy-start | bytes 983044
Sparse Core Ops, SparseCore 0:
  10.3 45.4 all-gather.3
  61.0 82.3 reduce-scatter.6
  146.4 49.2 all-gather.5
  200.6 64.8 reduce-scatter.8
  269.1 85.2 reduce-scatter.12
  357.3 51.4 all-gather.7
  470.5 67.5 reduce-scatter.10
